TPU v7x, 32 devices: a whole 2x2x4 slice. The times are simulated.
32 devices in a mesh: groups: 2 (over x), ctx: 8 (over z, y), head: 2 (over core).
Axes of the slice: x: 2, y: 2, z: 4, core: 2. Of those that a mesh axis runs over, the one named last changes fastest.
Arguments:
- query_nope: bfloat16 [32, 128, 128], P('groups', ('ctx', 'head')), parts along dimension 0, may hold values from -6 to 6
- query_rope: bfloat16 [32, 8192], P('groups', ('ctx', 'head')), parts along dimension 0, may hold values from -31 to 31
- key_absorb: bfloat16 [128, 128, 512], P(('ctx', 'head')), may hold values from -0.5 to 0.5
- value_absorb: bfloat16 [128, 512, 128], P(('ctx', 'head')), may hold values from -4 to 4
- output_weight: bfloat16 [16384, 7168], P(('ctx', 'head')), may hold values from -0.0625 to 0.0625
- latent_cache: bfloat16 [3584, 64, 576], P(('groups', 'ctx')), parts along dimension 0, may hold values from -4 to 4
- page_owner: int32 [3584], P(('groups', 'ctx')), parts along dimension 0, may hold values from -1 to 15, as said below
Outputs:
- layer_output: bfloat16 [32, 7168], P('groups', ('ctx', 'head')), parts along dimension 0
There are 2 independent parts, one for each index of `groups`. A program takes and returns all parts, laid end to end along the dimension named above; an argument that names none is the same for every part. Nothing has to cross between parts.
Inputs may be any that keep to these rules, and one draw needn't show every extreme that they name: `page_owner`: a slot's request, or -1 for an unused slot; every request owns at least one slot; every index of ctx has an eighth of its 224 slots or more in use, and some index has all 224 in use.
All inputs are finite; a program needn't handle non-finite values.
Results may differ from a plain program's by a relative error of at most 0.03.
Values may be sent and summed in bfloat16 or wider, within the bound.
A program may use at most 128 MiB of HBM per device.

v0:
```python
import jax
import jax.numpy as jnp
from jax import lax
from jax.sharding import PartitionSpec as P

BLOCK_PAGES = 8


masked_score = -1e30


def body(query_nope, query_rope, key_absorb, value_absorb, output_weight, latent_cache, page_owner):
    requests, heads_here, nope_size = query_nope.shape
    latent_size = key_absorb.shape[2]
    rope_size = query_rope.shape[1] // heads_here
    pages_here, page_len, entry_size = latent_cache.shape
    score_scale = (nope_size + rope_size) ** (-0.5)
    query_latent = jnp.einsum(
        "rhn,hnl->rhl", query_nope, key_absorb, preferred_element_type=jnp.float32
    ).astype(jnp.bfloat16)
    all_latent, all_rope = (
        lax.all_gather(query_latent, "ctx", axis=1, tiled=True),
        lax.all_gather(query_rope, "ctx", axis=1, tiled=True),
    )
    heads_ctx = all_latent.shape[1]
    query_full = jnp.concatenate(
        [all_latent, all_rope.reshape(requests, heads_ctx, rope_size)], axis=2
    )
    block_count = pages_here // BLOCK_PAGES
    cache_blocks = latent_cache.reshape(block_count, BLOCK_PAGES, page_len, entry_size)
    owner_blocks = page_owner.reshape(block_count, BLOCK_PAGES)
    request_ids = jnp.arange(requests, dtype=jnp.int32)

    def score_block(inputs):
        page_rows, owner_ids = inputs
        page_query = query_full[jnp.clip(owner_ids, 0, requests - 1)]
        scores = (
            jnp.einsum("ptk,phk->pth", page_rows, page_query, preferred_element_type=jnp.float32)
            * score_scale
        )
        return jnp.where((owner_ids >= 0)[:, None, None], scores, masked_score)

    block_scores = lax.map(score_block, (cache_blocks, owner_blocks))
    page_max = jnp.max(block_scores, axis=2).reshape(pages_here, heads_ctx)
    owner_hot = page_owner[:, None] == request_ids[None, :]
    local_max = jnp.max(
        jnp.where(owner_hot[:, :, None], page_max[:, None, :], masked_score), axis=0
    )

    def sum_block(state, inputs):
        running_sum, running_total = state
        page_rows, owner_ids, scores = inputs
        offset = local_max[jnp.clip(owner_ids, 0, requests - 1)]
        weights = jnp.where(
            (owner_ids >= 0)[:, None, None], jnp.exp(scores - offset[:, None, :]), 0.0
        )
        weight_half = weights.astype(jnp.bfloat16)
        page_out = jnp.einsum(
            "pth,ptl->phl",
            weight_half,
            page_rows[:, :, :latent_size],
            preferred_element_type=jnp.float32,
        )
        target = jnp.where(owner_ids >= 0, owner_ids, requests)
        running_sum = running_sum.at[target].add(page_out, mode="drop")
        running_total = running_total.at[target].add(jnp.sum(weights, axis=1), mode="drop")
        return ((running_sum, running_total), None)

    start_state = (
        jnp.zeros((requests, heads_ctx, latent_size), jnp.float32),
        jnp.zeros((requests, heads_ctx), jnp.float32),
    )
    (latent_sum, weight_total), _ = lax.scan(
        sum_block, start_state, (cache_blocks, owner_blocks, block_scores)
    )
    got_max, got_total, got_sum = (
        lax.all_to_all(
            local_max[None].astype(jnp.bfloat16), "ctx", split_axis=2, concat_axis=0, tiled=True
        ).astype(jnp.float32),
        lax.all_to_all(
            weight_total[None].astype(jnp.bfloat16), "ctx", split_axis=2, concat_axis=0, tiled=True
        ).astype(jnp.float32),
        lax.all_to_all(
            latent_sum[None].astype(jnp.bfloat16), "ctx", split_axis=2, concat_axis=0, tiled=True
        ).astype(jnp.float32),
    )
    top_max = jnp.max(got_max, axis=0)
    factor = jnp.exp(got_max - top_max[None])
    mine_total = jnp.sum(factor * got_total, axis=0)
    mine_sum = jnp.sum(factor[..., None] * got_sum, axis=0)
    attended = (mine_sum / mine_total[..., None]).astype(jnp.bfloat16)
    head_out = jnp.einsum(
        "rhl,hlv->rhv", attended, value_absorb, preferred_element_type=jnp.float32
    ).astype(jnp.bfloat16)
    partial_out = jnp.dot(
        head_out.reshape(requests, -1), output_weight, preferred_element_type=jnp.float32
    )
    return lax.psum_scatter(
        partial_out.astype(jnp.bfloat16), ("ctx", "head"), scatter_dimension=1, tiled=True
    )


def solution(mesh):
    return jax.shard_map(
        body,
        mesh=mesh,
        in_specs=(
            P("groups", ("ctx", "head"), None),
            P("groups", ("ctx", "head")),
            P(("ctx", "head"), None, None),
            P(("ctx", "head"), None, None),
            P(("ctx", "head"), None),
            P(("groups", "ctx"), None, None),
            P(("groups", "ctx")),
        ),
        out_specs=P("groups", ("ctx", "head")),
        check_vma=False,
    )
```

profile of v0, /device:TPU:0, one launch (start us, length us, event | category | flops | bytes accessed | tf_op | source)
XLA Modules:
  0.0 475.0 jit_solution(9024620244627577398)
XLA Ops:
  10.2 32.7 %all_gather.7 = bf16[16,4096]{1,0:T(8,128)(2,1)S(1)} all-gather(bf16[16,512]{1,0:T(8,128)(2,1)} %param.12), channel_id=1, replica_groups=mesh['groups'=2,'ctx'=8,'head'=2] {'ctx'}, dimensions={1}, use_global_device_ids=true | all-gather | bytes 147456 | tf_op jit(solution)/shard_map/all_gather | solution.py:23
  44.0 8.8 %all-gather.2.cloned.1.call-done = bf16[16,64,512]{2,0,1:T(8,128)(2,1)} async-done(((bf16[16,8,512]{2,0,1:T(8,128)(2,1)}), bf16[16,64,512]{2,0,1:T(8,128)(2,1)}) %all-gather.2.cloned.1.call-update) | async-done | bytes 1048592 | tf_op jit(solution)/shard_map/all_gather | solution.py:22
  54.5 80.9 %while.22 = (s32[]{:T(128)}, f32[28,8,64,64]{3,2,1,0:T(8,128)}, s32[28,8]{1,0:T(8,128)S(1)}, bf16[28,8,64,576]{3,2,1,0:T(8,128)(2,1)}, bf16[16,64,576]{2,1,0:T(8,128)(2,1)S(1)}, /*index=5*/s32[]{:T(128)}) while((s32[]{:T(128)}, f32[28,8,64,64]{3,2,1,0:T(8,128)}, s32[28,8]{1,0:T(8,128)S(1)}, bf16[28,8,64,576]{3,2,1,0:T(8,128)(2,1)}, ...), condition=%wide.region_1.2_spmd, body=%wide.region_0.1_spmd.sunk | while | flops 37815336 | bytes 2692349 | solution.py:43
  135.4 4.8 %reduce_max.32 = f32[28,8,64]{2,1,0:T(8,128)S(1)} reduce(f32[28,8,64,64]{3,2,1,0:T(8,128)} %get-tuple-element.285, f32[]{:T(128)} %constant.33.clone.1), dimensions={2}, to_apply=%region_2.3 | reduce | flops 903168 | bytes 3727364 | tf_op jit(solution)/shard_map/reduce_max | solution.py:44
  142.2 201.1 %while.23 = (s32[]{:T(128)}, f32[16,64,512]{2,1,0:T(8,128)}, f32[16,64]{1,0:T(8,128)S(1)}, s32[28,8]{1,0:T(8,128)S(1)}, f32[28,8,64,64]{3,2,1,0:T(8,128)}, /*ind...) while((s32[]{:T(128)}, f32[16,64,512]{2,1,0:T(8,128)}, f32[16,64]{1,0:T(8,128)S(1)}, ...), condition=%wide.region_9.10_spmd, body=%wide.region_5.9_spmd.sunk | while | flops 34014288 | bytes 6839157 | solution.py:73
  145.4 3.2 scatter_fusion
  152.8 3.3 scatter_fusion
  160.2 3.3 scatter_fusion
  167.7 3.2 scatter_fusion
  175.0 3.0 scatter_fusion
  182.1 3.0 scatter_fusion
  189.3 3.0 scatter_fusion
  203.6 3.0 scatter_fusion
  210.7 3.0 scatter_fusion
  225.0 3.0 scatter_fusion
  232.2 3.0 scatter_fusion
  246.5 3.0 scatter_fusion
  253.6 3.0 scatter_fusion
  267.9 3.0 scatter_fusion
  275.0 3.0 scatter_fusion
  289.3 3.0 scatter_fusion
  296.5 3.0 scatter_fusion
  310.8 3.0 scatter_fusion
  317.9 3.0 scatter_fusion
  344.0 8.4 %all-to-all-start.2 = ((bf16[1,16,64]{1,0,2:T(2,128)(2,1)}), bf16[1,16,64]{1,0,2:T(2,128)(2,1)S(1)}, u32[]{:S(2)}, u32[]{:S(2)}) async-start(bf16[1,16,64]{1,0,2:T(2,128)(2,1)} %copy.78), calls=%async_computation.2 | async-start | bytes 65536 | tf_op jit(solution)/shard_map/all_to_all | solution.py:80
  353.1 6.0 %all-to-all-done.2 = bf16[1,16,64]{1,0,2:T(2,128)(2,1)S(1)} async-done(((bf16[1,16,64]{1,0,2:T(2,128)(2,1)}), bf16[1,16,64]{1,0,2:T(2,128)(2,1)S(1)}, u32[]{:S(2)}, u32[]{:S(2)}) %all-to-all-start.2) | async-done | bytes 2080 | tf_op jit(solution)/shard_map/all_to_all | solution.py:80
  359.1 3.3 all-to-all-start
  362.4 3.7 copy.104
  369.0 3.6 all-to-all-start.1
  372.9 22.7 %all-to-all-done.1 = bf16[1,16,64,512]{3,1,0,2:T(8,128)(2,1)S(1)} async-done(((bf16[1,16,64,512]{3,1,0,2:T(8,128)(2,1)}), bf16[1,16,64,512]{3,1,0,2:T(8,128)(2,1)S(1)}, u32[]{:S(2)}, u32[]{:S(2)}) %all-to-all-start.1) | async-done | bytes 1048608 | tf_op jit(solution)/shard_map/all_to_all | solution.py:83
  397.5 7.2 %convolution_convert_fusion = bf16[16,7168]{1,0:T(8,128)(2,1)S(1)} fusion(bf16[1024,7168]{1,0:T(8,128)(2,1)} %param.15, bf16[8,2,8,128]{3,2,1,0:T(8,128)(2,1)S(1)} %fusion.22), kind=kOutput, calls=%fused_computation.38 | convolution fusion | flops 234995712 | bytes 14942208 | tf_op jit(solution)/shard_map/dot_general | solution.py:95
  406.4 60.2 %reduce-scatter.4.cloned.1.call-done = bf16[448,16]{1,0:T(8,128)(2,1)} async-done(((bf16[7168,16]{1,0:T(8,128)(2,1)}), bf16[448,16]{1,0:T(8,128)(2,1)}) %reduce-scatter.4.cloned.1.call-update) | async-done | bytes 14352
  (465 shorter events, 239.9 us)
Async XLA Ops:
  6.5 1.2 copy-start
  6.5 46.3 %all-gather.2.cloned.1.call-start = ((), (), s32[]{:S(2)}) async-start(), calls=%async_computation.4 | async-start | bytes 1179648 | tf_op jit(solution)/shard_map/all_gather | solution.py:22
  344.0 15.1 %all-to-all-start.2 = ((bf16[1,16,64]{1,0,2:T(2,128)(2,1)}), bf16[1,16,64]{1,0,2:T(2,128)(2,1)S(1)}, u32[]{:S(2)}, u32[]{:S(2)}) async-start(bf16[1,16,64]{1,0,2:T(2,128)(2,1)} %copy.78), calls=%async_computation.2 | async-start | bytes 65536 | tf_op jit(solution)/shard_map/all_to_all | solution.py:80
  359.1 10.0 %all-to-all-start = ((bf16[1,16,64]{1,0,2:T(2,128)(2,1)}), bf16[1,16,64]{1,0,2:T(2,128)(2,1)S(1)}, u32[]{:S(2)}, u32[]{:S(2)}) async-start(bf16[1,16,64]{1,0,2:T(2,128)(2,1)} %copy.73), calls=%async_computation | async-start | bytes 65536 | tf_op jit(solution)/shard_map/all_to_all | solution.py:77
  369.0 26.6 %all-to-all-start.1 = ((bf16[1,16,64,512]{3,1,0,2:T(8,128)(2,1)}), bf16[1,16,64,512]{3,1,0,2:T(8,128)(2,1)S(1)}, u32[]{:S(2)}, u32[]{:S(2)}) async-start(bf16[1,16,64,512]{3,1,0,2:T(8,128)(2,1)} %bitcast.86), calls=%async_computation.1 | async-start | bytes 2097152 | tf_op jit(solution)/shard_map/all_to_all | solution.py:83
  372.6 94.0 %reduce-scatter.4.cloned.1.call-start = ((), (), s32[]{:S(2)}) async-start(), calls=%async_computation.5 | async-start | bytes 1949696
  395.6 1.7 copy-start.1
Sparse Core Ops, SparseCore 0:
  9.6 43.2 all-gather.1
  406.5 60.0 reduce-scatter.3
where the time goes:
time: 480 us; the launch traced here: 475 us
  other arithmetic  120 us (25%)
  local copies, waits for them, and re-layouts  110 us (23%)
  waiting for transfers between devices  101 us (21%)
  matrix products  79.9 us (17%)
  blocking collectives  32.7 us (7%)
  starting transfers between devices  15.3 us (3%)
  between operations  13.6 us (3%)
    scatter-add x28, other arithmetic, sum_block(): running_sum = running_sum.at[target].add(page_out, mode='drop')  84.1 us
    dot_general x28, matrix products, score_block(): jnp.einsum('ptk,phk->pth', page_rows, page_query, preferred_element_type=...  60.8 us
    unnamed x3, waiting for transfers between devices  60.2 us
    all_gather x1, blocking collectives, body(): lax.all_gather(query_rope, 'ctx', axis=1, tiled=True)  32.7 us
    squeeze x28, local copies, waits for them, and re-layouts, body(): block_scores = lax.map(score_block, (cache_blocks, owner_blocks))  32.2 us
    dynamic_slice x56, local copies, waits for them, and re-layouts, body(): lax.scan(sum_block, start_state, (cache_blocks, owner_blocks, block_scores))  30.9 us
    all_to_all x1, waiting for transfers between devices, body(): lax.all_to_all(latent_sum[None].astype(jnp.bfloat16), 'ctx', split_axis=2...  22.7 us
    gather x28, local copies, waits for them, and re-layouts, score_block(): page_query = query_full[jnp.clip(owner_ids, 0, requests - 1)]  18.6 us
  transfers between devices with their start and end apart: 5, of which 5 were waited for; matrix products, arithmetic and copies ran while one was open for 1% of the time, Pallas kernels for 0%

commit v1 on v0

v1 whole, which is shorter than its diff:
```python
import functools

import jax
import jax.numpy as jnp
from jax import lax
from jax.experimental import pallas as pl
from jax.experimental.pallas import tpu as pltpu
from jax.sharding import PartitionSpec as P

F32 = jnp.float32
BF16 = jnp.bfloat16


def dot_nt(a, b):
    return lax.dot_general(a, b, (((1,), (1,)), ((), ())), preferred_element_type=F32)


def attention_kernel(heads_here, group, score_scale, owner_ref, q_ref, cache_ref, sum_ref, stat_ref,
                     pages, query, scores, peak, total, acc, sems):
    ctx = q_ref.shape[0]
    slots, heads, _ = acc.shape
    requests = slots - 1
    page_count, page_len, _ = pages.shape
    latent = acc.shape[2]
    chunks = sems.shape[0]
    chunk = page_count // chunks

    def fetch(i):
        window = pl.ds(i * chunk, chunk)
        return pltpu.make_async_copy(cache_ref.at[window], pages.at[window], sems.at[i])

    for i in range(chunks):
        fetch(i).start()
    for r in range(requests):
        rows = [q_ref[c, r * heads_here:(r + 1) * heads_here, :].astype(F32) for c in range(ctx)]
        query[r] = jnp.concatenate(rows, axis=0).astype(BF16)
    peak[...] = jnp.full_like(peak, -1e30)
    total[...] = jnp.zeros_like(total)
    acc[...] = jnp.zeros_like(acc)

    def score_group(base):
        found = []
        for j in range(group):
            owner = owner_ref[base + j]
            found.append(dot_nt(query[jnp.minimum(owner, requests - 1)], pages[base + j]) * score_scale)
        for j in range(group):
            owner = owner_ref[base + j]
            scores[base + j] = found[j]
            peak[owner] = jnp.maximum(peak[owner], found[j])

    @pl.loop(0, chunks)
    def _(i):
        fetch(i).wait()

        @pl.loop(0, chunk // group)
        def _(g):
            score_group(i * chunk + g * group)

    for r in range(slots):
        peak[r] = jnp.broadcast_to(jnp.max(peak[r], axis=1, keepdims=True), peak.shape[1:])

    @pl.loop(0, page_count // group)
    def _(g):
        base = g * group
        parts = []
        for j in range(group):
            owner = owner_ref[base + j]
            weight = jnp.exp(scores[base + j] - peak[owner])
            total[owner] = total[owner] + weight
            parts.append(jnp.dot(weight.astype(BF16), pages[base + j, :, :latent], preferred_element_type=F32))
        for j in range(group):
            owner = owner_ref[base + j]
            acc[owner] = acc[owner] + parts[j]

    lane = lax.broadcasted_iota(jnp.int32, stat_ref.shape, 1)
    stats = jnp.zeros(stat_ref.shape, F32)
    for r in range(requests):
        stats = jnp.where(lane == r, jnp.max(peak[r], axis=1, keepdims=True), stats)
        stats = jnp.where(lane == requests + r, jnp.sum(total[r], axis=1, keepdims=True), stats)
    stat_ref[...] = stats
    for c in range(ctx):
        part = acc[:requests, c * heads_here:(c + 1) * heads_here, :]
        sum_ref[c] = part.reshape(requests * heads_here, latent).astype(BF16)


def attention(gathered, cache, owners, requests, heads_here, latent, score_scale):
    ctx, _, entry = gathered.shape
    page_count, page_len, _ = cache.shape
    heads = ctx * heads_here
    chunks = next(n for n in (14, 8, 7, 4, 2, 1) if page_count % n == 0)
    group = next(n for n in (8, 4, 2, 1) if (page_count // chunks) % n == 0)
    return pl.pallas_call(
        functools.partial(attention_kernel, heads_here, group, score_scale),
        grid_spec=pltpu.PrefetchScalarGridSpec(
            num_scalar_prefetch=1,
            grid=(1,),
            in_specs=[
                pl.BlockSpec(gathered.shape, lambda i, o: (0, 0, 0), pipeline_mode=pl.Buffered(1)),
                pl.BlockSpec(memory_space=pl.ANY),
            ],
            out_specs=[
                pl.BlockSpec((ctx, requests * heads_here, latent), lambda i, o: (0, 0, 0), pipeline_mode=pl.Buffered(1)),
                pl.BlockSpec((heads, 128), lambda i, o: (0, 0), pipeline_mode=pl.Buffered(1)),
            ],
            scratch_shapes=[
                pltpu.VMEM((page_count, page_len, entry), BF16),
                pltpu.VMEM((requests, heads, entry), BF16),
                pltpu.VMEM((page_count, heads, page_len), F32),
                pltpu.VMEM((requests + 1, heads, page_len), F32),
                pltpu.VMEM((requests + 1, heads, page_len), F32),
                pltpu.VMEM((requests + 1, heads, latent), F32),
                pltpu.SemaphoreType.DMA((chunks,)),
            ],
        ),
        out_shape=[
            jax.ShapeDtypeStruct((ctx, requests * heads_here, latent), BF16),
            jax.ShapeDtypeStruct((heads, 128), F32),
        ],
        compiler_params=pltpu.CompilerParams(vmem_limit_bytes=48 << 20),
    )(owners, gathered, cache)


def body(query_nope, query_rope, key_absorb, value_absorb, output_weight, latent_cache, page_owner):
    requests, heads_here, nope_size = query_nope.shape
    latent_size = key_absorb.shape[2]
    rope_size = query_rope.shape[1] // heads_here
    score_scale = (nope_size + rope_size) ** (-0.5)
    query_latent = jnp.einsum(
        "rhn,hnl->rhl", query_nope, key_absorb, preferred_element_type=F32
    ).astype(BF16)
    query_mine = jnp.concatenate(
        [query_latent, query_rope.reshape(requests, heads_here, rope_size)], axis=2
    ).reshape(requests * heads_here, -1)
    gathered = lax.all_gather(query_mine, "ctx", axis=0, tiled=False)
    owners = jnp.where(page_owner < 0, requests, page_owner)
    sums, stats = attention(gathered, latent_cache, owners, requests, heads_here, latent_size, score_scale)
    ctx = gathered.shape[0]
    got_sum = lax.all_to_all(sums, "ctx", split_axis=0, concat_axis=0, tiled=True).reshape(
        ctx, requests, heads_here, latent_size).astype(F32)
    got_stat = lax.all_to_all(
        stats.reshape(ctx, heads_here, -1), "ctx", split_axis=0, concat_axis=0, tiled=True)
    got_max = got_stat[:, :, :requests].transpose(0, 2, 1)
    got_total = got_stat[:, :, requests:2 * requests].transpose(0, 2, 1)
    top_max = jnp.max(got_max, axis=0)
    factor = jnp.exp(got_max - top_max[None])
    mine_total = jnp.sum(factor * got_total, axis=0)
    mine_sum = jnp.sum(factor[..., None] * got_sum, axis=0)
    attended = (mine_sum / mine_total[..., None]).astype(BF16)
    head_out = jnp.einsum(
        "rhl,hlv->rhv", attended, value_absorb, preferred_element_type=F32
    ).astype(BF16)
    partial_out = jnp.dot(
        head_out.reshape(requests, -1), output_weight, preferred_element_type=F32
    )
    return lax.psum_scatter(
        partial_out.astype(BF16), ("ctx", "head"), scatter_dimension=1, tiled=True
    )


def solution(mesh):
    return jax.shard_map(
        body,
        mesh=mesh,
        in_specs=(
            P("groups", ("ctx", "head"), None),
            P("groups", ("ctx", "head")),
            P(("ctx", "head"), None, None),
            P(("ctx", "head"), None, None),
            P(("ctx", "head"), None),
            P(("groups", "ctx"), None, None),
            P(("groups", "ctx")),
        ),
        out_specs=P("groups", ("ctx", "head")),
        check_vma=False,
    )
```

time: 480 us -> 192 us (0.40); the launches traced: 475 us -> 192 us
  other arithmetic: 120 us -> 0.47 us
  local copies, waits for them, and re-layouts: 110 us -> 8.07 us
  matrix products: 79.9 us -> 8.46 us
  waiting for transfers between devices: 101 us -> 126 us
  blocking collectives: 32.7 us -> 9.89 us
  Pallas kernels: 0 us -> 21.7 us
  starting transfers between devices: 15.3 us -> 3.6 us
    scatter-add x56 -> x0, other arithmetic: 101 us -> none  [the longest x28 84.1 us: sum_block(): running_sum = running_sum.at[target].add(page_out, mode='drop')]
    dot_general x56 -> x0, matrix products: 70.8 us -> none  [the longest x28 60.8 us: score_block(): jnp.einsum('ptk,phk->pth', page_rows, page_query, preferred_element_type=...]
    all_gather x1, waiting for transfers between devices: 8.8 us -> 44 us  [body(): gathered = lax.all_gather(query_mine, 'ctx', axis=0, tiled=False)]
    gather x56 -> x0, local copies, waits for them, and re-layouts: 34.2 us -> none  [the longest x28 18.6 us: score_block(): page_query = query_full[jnp.clip(owner_ids, 0, requests - 1)]]
    all_gather x1 -> x0, blocking collectives: 32.7 us -> none  [body(): lax.all_gather(query_rope, 'ctx', axis=1, tiled=True)]
    squeeze x28 -> x0, local copies, waits for them, and re-layouts: 32.2 us -> none  [body(): block_scores = lax.map(score_block, (cache_blocks, owner_blocks))]
    dynamic_slice x56 -> x0, local copies, waits for them, and re-layouts: 30.9 us -> none  [body(): lax.scan(sum_block, start_state, (cache_blocks, owner_blocks, block_scores))]
    pallas_call x0 -> x1, Pallas kernels: none -> 21.7 us  [attention(): pl.pallas_call(functools.partial(attention_kernel, heads_here, group, sco...]
  transfers between devices with their start and end apart: 5 -> 3, of which waited for: 5 -> 3; matrix products, arithmetic and copies ran while one was open for 1% -> 0% of each run, Pallas kernels for 0% -> 0%
where the time goes in v1:
time: 192 us
  waiting for transfers between devices  126 us (66%)
  Pallas kernels  21.7 us (11%)
  between operations  13.5 us (7%)
  blocking collectives  9.89 us (5%)
  matrix products  8.46 us (4%)
  local copies, waits for them, and re-layouts  8.07 us (4%)
  starting transfers between devices  3.6 us (2%)
    unnamed x3, waiting for transfers between devices  59.7 us
    all_gather x1, waiting for transfers between devices, body(): gathered = lax.all_gather(query_mine, 'ctx', axis=0, tiled=False)  44 us
    all_to_all x1, waiting for transfers between devices, body(): lax.all_to_all(sums, 'ctx', split_axis=0, concat_axis=0, tiled=True)  22.7 us
    pallas_call x1, Pallas kernels, attention(): pl.pallas_call(functools.partial(attention_kernel, heads_here, group, sco...  21.7 us
    all_to_all x1, blocking collectives, body(): lax.all_to_all(stats.reshape(ctx, heads_here, -1), 'ctx', split_axis=0, c...  9.89 us
    dot_general x1, matrix products, body(): jnp.dot(head_out.reshape(requests, -1), output_weight, preferred_element_...  7.2 us
    unnamed x8, local copies, waits for them, and re-layouts  4.44 us
  transfers between devices with their start and end apart: 3, of which 3 were waited for; matrix products, arithmetic and copies ran while one was open for 0% of the time, Pallas kernels for 0%

profile of v1, /device:TPU:0, one launch (start us, length us, event | category | flops | bytes accessed | tf_op | source)
XLA Modules:
  0.0 192.0 jit_solution(13169696252541208938)
XLA Ops:
  6.5 0.0 copy-start
  6.5 0.0 copy-start.2
  6.5 0.0 all-gather.2.cloned.1.call-start
  6.5 1.2 copy-done
  7.8 1.0 fusion
  8.7 0.1 copy.48
  8.9 0.8 concatenate.9
  9.7 0.8 copy.30
  10.5 0.0 all-gather.2.cloned.1.call-update
  10.5 0.0 copy-done.2
  10.5 44.0 %all-gather.2.cloned.1.call-done = bf16[8,128,576]{1,2,0:T(8,128)(2,1)} async-done(((bf16[1,128,576]{1,2,0:T(8,128)(2,1)}), bf16[8,128,576]{1,2,0:T(8,128)(2,1)}) %all-gather.2.cloned.1.call-update) | async-done | bytes 1179664 | tf_op jit(solution)/shard_map/all_gather | solution.py:134
  54.5 1.7 copy.31.q_ref
  56.2 21.7 %shard_map.73 = (bf16[8,128,512]{2,1,0:T(8,128)(2,1)}, f32[64,128]{1,0:T(8,128)S(1)}) custom-call(s32[224]{0:T(256)S(1)} %compare_select_fusion.owner_ref, bf16[8,128,576]{2,1,0:T(8,128)(2,1)S(1)} %copy.31.q_ref, bf16[224,64,576]{2,1,0:T(8,128)(2,1)} %cache_ref.1), custom_call_target="tpu_custom_call" | custom-call | tf_op jit(solution)/shard_map/pallas_call | solution.py:92
  77.9 0.0 copy-start.1
  77.9 9.9 %all_to_all.10 = f32[8,8,128]{2,1,0:T(8,128)S(1)} all-to-all(f32[8,8,128]{2,1,0:T(8,128)S(1)} %bitcast.34), channel_id=1, replica_groups=mesh['groups'=2,'ctx'=8,'head'=2] {'ctx'}, dimensions={0} | all-to-all | bytes 65536 | tf_op jit(solution)/shard_map/all_to_all | solution.py:140
  87.8 3.6 %all-to-all-start.1 = ((bf16[8,128,512]{2,1,0:T(8,128)(2,1)}), bf16[8,128,512]{2,1,0:T(8,128)(2,1)S(1)}, u32[]{:S(2)}, u32[]{:S(2)}) async-start(bf16[8,128,512]{2,1,0:T(8,128)(2,1)} %get-tuple-element.8), calls=%async_computation.1 | async-start | bytes 2097152 | tf_op jit(solution)/shard_map/all_to_all | solution.py:138
  91.4 0.0 reduce-scatter.4.cloned.1.call-start
  91.4 0.1 fusion.7
  91.5 0.1 copy.32
  91.6 0.1 mul.14
  91.7 0.1 copy.33
  91.8 22.7 %all-to-all-done.1 = bf16[8,128,512]{2,1,0:T(8,128)(2,1)S(1)} async-done(((bf16[8,128,512]{2,1,0:T(8,128)(2,1)}), bf16[8,128,512]{2,1,0:T(8,128)(2,1)S(1)}, u32[]{:S(2)}, u32[]{:S(2)}) %all-to-all-start.1) | async-done | bytes 1048608 | tf_op jit(solution)/shard_map/all_to_all | solution.py:138
  114.4 0.3 multiply_reduce_fusion
  114.7 0.1 fusion.2
  114.8 0.0 copy-done.1
  114.8 0.3 fusion.1
  115.1 7.2 %convolution_convert_fusion = bf16[16,7168]{1,0:T(8,128)(2,1)S(1)} fusion(bf16[1024,7168]{1,0:T(8,128)(2,1)} %param.11, bf16[8,2,8,128]{3,2,1,0:T(8,128)(2,1)S(1)} %fusion.1), kind=kOutput, calls=%fused_computation | convolution fusion | flops 234995712 | bytes 14942208 | tf_op jit(solution)/shard_map/dot_general | solution.py:152
  122.3 1.6 copy.36
  123.9 0.0 reduce-scatter.4.cloned.1.call-update
  124.0 59.7 %reduce-scatter.4.cloned.1.call-done = bf16[448,16]{1,0:T(8,128)(2,1)} async-done(((bf16[7168,16]{1,0:T(8,128)(2,1)}), bf16[448,16]{1,0:T(8,128)(2,1)}) %reduce-scatter.4.cloned.1.call-update) | async-done | bytes 14352
  183.6 1.6 copy.37
  (3 shorter events, 0.0 us)
Async XLA Ops:
  6.5 1.2 copy-start
  6.5 4.0 %copy-start.2 = (s32[224]{0:T(256)S(1)}, s32[224]{0:T(256)}, u32[]{:S(2)}) copy-start(s32[224]{0:T(256)} %param.13) | copy-start | bytes 2692
  6.5 48.0 %all-gather.2.cloned.1.call-start = ((), (), s32[]{:S(2)}) async-start(), calls=%async_computation.3 | async-start | bytes 1327104 | tf_op jit(solution)/shard_map/all_gather | solution.py:134
  77.9 36.9 %copy-start.1 = (bf16[8,512,128]{2,1,0:T(8,128)(2,1)S(1)}, bf16[8,512,128]{2,1,0:T(8,128)(2,1)}, u32[]{:S(2)}) copy-start(bf16[8,512,128]{2,1,0:T(8,128)(2,1)} %param.10) | copy-start | bytes 3145732
  87.8 26.7 %all-to-all-start.1 = ((bf16[8,128,512]{2,1,0:T(8,128)(2,1)}), bf16[8,128,512]{2,1,0:T(8,128)(2,1)S(1)}, u32[]{:S(2)}, u32[]{:S(2)}) async-start(bf16[8,128,512]{2,1,0:T(8,128)(2,1)} %get-tuple-element.8), calls=%async_computation.1 | async-start | bytes 2097152 | tf_op jit(solution)/shard_map/all_to_all | solution.py:138
  91.4 92.3 %reduce-scatter.4.cloned.1.call-start = ((), (), s32[]{:S(2)}) async-start(), calls=%async_computation.4 | async-start | bytes 1949696
Sparse Core Ops, SparseCore 0:
  10.6 43.8 all-gather.1
  124.1 59.4 reduce-scatter.3

commit v2 on v1

--- a/solution.py
+++ b/solution.py
@@ -72,21 +72,26 @@
             owner = owner_ref[base + j]
             acc[owner] = acc[owner] + parts[j]
 
-    lane = lax.broadcasted_iota(jnp.int32, stat_ref.shape, 1)
-    stats = jnp.zeros(stat_ref.shape, F32)
+    lane = lax.broadcasted_iota(jnp.int32, (heads, stat_ref.shape[-1]), 1)
+    top = jnp.zeros(lane.shape, F32)
+    norm = jnp.zeros(lane.shape, F32)
     for r in range(requests):
-        stats = jnp.where(lane == r, jnp.max(peak[r], axis=1, keepdims=True), stats)
-        stats = jnp.where(lane == requests + r, jnp.sum(total[r], axis=1, keepdims=True), stats)
-    stat_ref[...] = stats
+        top = jnp.where(lane == r, jnp.max(peak[r], axis=1, keepdims=True), top)
+        norm = jnp.where(lane == r, jnp.sum(total[r], axis=1, keepdims=True), norm)
     for c in range(ctx):
-        part = acc[:requests, c * heads_here:(c + 1) * heads_here, :]
-        sum_ref[c] = part.reshape(requests * heads_here, latent).astype(BF16)
+        rows = slice(c * heads_here, (c + 1) * heads_here)
+        part = acc[:requests, rows, :]
+        sum_ref[c % 2, c // 2] = part.reshape(requests * heads_here, latent).astype(BF16)
+        stat_ref[c % 2, c // 2, 0] = top[rows]
+        stat_ref[c % 2, c // 2, 1] = norm[rows]
 
 
 def attention(gathered, cache, owners, requests, heads_here, latent, score_scale):
     ctx, _, entry = gathered.shape
     page_count, page_len, _ = cache.shape
     heads = ctx * heads_here
+    sum_shape = (2, ctx // 2, requests * heads_here, latent)
+    stat_shape = (2, ctx // 2, 2, heads_here, 128)
     chunks = next(n for n in (14, 8, 7, 4, 2, 1) if page_count % n == 0)
     group = next(n for n in (8, 4, 2, 1) if (page_count // chunks) % n == 0)
     return pl.pallas_call(
@@ -99,8 +104,8 @@
                 pl.BlockSpec(memory_space=pl.ANY),
             ],
             out_specs=[
-                pl.BlockSpec((ctx, requests * heads_here, latent), lambda i, o: (0, 0, 0), pipeline_mode=pl.Buffered(1)),
-                pl.BlockSpec((heads, 128), lambda i, o: (0, 0), pipeline_mode=pl.Buffered(1)),
+                pl.BlockSpec(sum_shape, lambda i, o: (0,) * 4, pipeline_mode=pl.Buffered(1)),
+                pl.BlockSpec(stat_shape, lambda i, o: (0,) * 5, pipeline_mode=pl.Buffered(1)),
             ],
             scratch_shapes=[
                 pltpu.VMEM((page_count, page_len, entry), BF16),
@@ -113,53 +118,311 @@
             ],
         ),
         out_shape=[
-            jax.ShapeDtypeStruct((ctx, requests * heads_here, latent), BF16),
-            jax.ShapeDtypeStruct((heads, 128), F32),
+            jax.ShapeDtypeStruct(sum_shape, BF16),
+            jax.ShapeDtypeStruct(stat_shape, F32),
         ],
         compiler_params=pltpu.CompilerParams(vmem_limit_bytes=48 << 20),
     )(owners, gathered, cache)
 
 
-def body(query_nope, query_rope, key_absorb, value_absorb, output_weight, latent_cache, page_owner):
+def remote(src, dst, send_sem, recv_sem, where):
+    return pltpu.make_async_remote_copy(
+        src_ref=src, dst_ref=dst, send_sem=send_sem, recv_sem=recv_sem,
+        device_id=where, device_id_type=pl.DeviceIdType.MESH)
+
+
+def gather_kernel(nz, nope_ref, rope_ref, key_ref, out_ref, wide, rows, mine,
+                  y_send, y_recv, up_send, up_recv, down_send, down_recv):
+    requests, heads_here, _ = nope_ref.shape
+    latent = key_ref.shape[2]
+    rope = rope_ref.shape[1] // heads_here
+    me = lax.axis_index("ctx")
+    z, y = me // 2, me % 2
+    partner = {"ctx": z * 2 + 1 - y}
+    above, below = {"ctx": me + 2}, {"ctx": me - 2}
+    has_above, has_below = z + 1 < nz, z > 0
+
+    barrier = pltpu.get_barrier_semaphore()
+    pl.semaphore_signal(barrier, inc=1, device_id=partner, device_id_type=pl.DeviceIdType.MESH)
+
+    @pl.when(has_above)
+    def _():
+        pl.semaphore_signal(barrier, inc=1, device_id=above, device_id_type=pl.DeviceIdType.MESH)
+
+    @pl.when(has_below)
+    def _():
+        pl.semaphore_signal(barrier, inc=1, device_id=below, device_id_type=pl.DeviceIdType.MESH)
+
+    wide[...] = nope_ref[...].astype(F32)
+    for h in range(heads_here):
+        rows[:, h, :latent] = jnp.dot(wide[:, h, :].astype(BF16), key_ref[h], preferred_element_type=F32)
+        rows[:, h, latent:] = rope_ref[:, h * rope:(h + 1) * rope].astype(F32)
+    value = rows[...].reshape(requests * heads_here, latent + rope).astype(BF16)
+    mine[...] = value
+    out_ref[me] = value
+
+    pl.semaphore_wait(barrier, 1 + has_above.astype(jnp.int32) + has_below.astype(jnp.int32))
+
+    def across(origin, src):
+        slot = out_ref.at[origin * 2 + y]
+        return remote(slot if src is None else src, slot, y_send.at[origin], y_recv.at[origin], partner)
+
+    def upward(step, src=None):
+        slot = out_ref.at[me - 2 * step]
+        return remote(slot if src is None else src, slot, up_send.at[step], up_recv.at[step], above)
+
+    def downward(step, src=None):
+        slot = out_ref.at[me + 2 * step]
+        return remote(slot if src is None else src, slot, down_send.at[step], down_recv.at[step], below)
+
+    def arrival(slot, sem):
+        return remote(slot, slot, sem, sem, partner)
+
+    @pl.when(has_above)
+    def _():
+        upward(0, mine).start()
+
+    @pl.when(has_below)
+    def _():
+        downward(0, mine).start()
+
+    across(z, mine).start()
+    for step in range(nz - 1):
+        @pl.when(z - 1 - step >= 0)
+        def _():
+            arrival(out_ref.at[me - 2 * (step + 1)], up_recv.at[step]).wait_recv()
+            if step + 1 < nz - 1:
+                @pl.when(has_above)
+                def _():
+                    upward(step + 1).start()
+            across(z - 1 - step, None).start()
+
+        @pl.when(z + 1 + step < nz)
+        def _():
+            arrival(out_ref.at[me + 2 * (step + 1)], down_recv.at[step]).wait_recv()
+            if step + 1 < nz - 1:
+                @pl.when(has_below)
+                def _():
+                    downward(step + 1).start()
+            across(z + 1 + step, None).start()
+
+    for origin in range(nz):
+        across(origin, mine).wait_send()
+        arrival(out_ref.at[origin * 2 + 1 - y], y_recv.at[origin]).wait_recv()
+    for step in range(nz - 1):
+        @pl.when(has_above & (z - step >= 0))
+        def _():
+            upward(step, mine).wait_send()
+
+        @pl.when(has_below & (z + step < nz))
+        def _():
+            downward(step, mine).wait_send()
+
+
+def gather_queries(query_nope, query_rope, key_absorb, ctx):
+    requests, heads_here, nope = query_nope.shape
+    entry = key_absorb.shape[2] + query_rope.shape[1] // heads_here
+    nz = ctx // 2
+    vmem = pl.BlockSpec(memory_space=pltpu.VMEM)
+    dma = pltpu.SemaphoreType.DMA
+    return pl.pallas_call(
+        functools.partial(gather_kernel, nz),
+        out_shape=jax.ShapeDtypeStruct((ctx, requests * heads_here, entry), BF16),
+        in_specs=[vmem] * 3,
+        out_specs=vmem,
+        scratch_shapes=[
+            pltpu.VMEM(query_nope.shape, F32),
+            pltpu.VMEM((requests, heads_here, entry), F32),
+            pltpu.VMEM((requests * heads_here, entry), BF16),
+            dma((nz,)), dma((nz,)), dma((nz,)), dma((nz,)), dma((nz,)), dma((nz,)),
+        ],
+        compiler_params=pltpu.CompilerParams(collective_id=0, has_side_effects=True, vmem_limit_bytes=16 << 20),
+    )(query_nope, query_rope, key_absorb)
+
+
+def project_kernel(ctx, sum_ref, stat_ref, value_ref, weight_ref, out_ref,
+                   weight, y_sum, y_stat, c_sum, c_stat, z_sum, z_stat, wide,
+                   h_keep, h_out, h_in, p_out, p_in,
+                   w_sem, ys_send, ys_recv, yt_send, yt_recv, zs_send, zs_recv, zt_send, zt_recv,
+                   h_send, h_recv, p_send, p_recv):
+    nz = ctx // 2
+    requests, half = out_ref.shape
+    block = 2 * half
+    heads_here = value_ref.shape[0]
+    latent = value_ref.shape[1]
+    me, core = lax.axis_index("ctx"), lax.axis_index("head")
+    z, y = me // 2, me % 2
+    partner, twin = {"ctx": z * 2 + 1 - y}, {"head": 1 - core}
+
+    barrier = pltpu.get_barrier_semaphore()
+    for k in range(1, ctx):
+        pl.semaphore_signal(barrier, inc=1, device_id={"ctx": (me + k) % ctx}, device_id_type=pl.DeviceIdType.MESH)
+    pl.semaphore_signal(barrier, inc=1, device_id=twin, device_id_type=pl.DeviceIdType.MESH)
+    load = pltpu.make_async_copy(weight_ref, weight, w_sem)
+    load.start()
+    pl.semaphore_wait(barrier, ctx)
+
+    stat_copy = remote(stat_ref.at[1 - y], y_stat, yt_send, yt_recv, partner)
+    stat_copy.start()
+    y_copies = []
+    for k in range(nz):
+        target = (z + 1 + k) % nz
+        copy = remote(sum_ref.at[1 - y, target], y_sum.at[k], ys_send.at[k], ys_recv.at[k], partner)
+        copy.start()
+        y_copies.append(copy)
+    stat_copy.wait_recv()
+
+    def spread(factor):
+        return jnp.concatenate([factor[:, r:r + 1] for r in range(requests)], axis=0)
+
+    z_copies = []
+    for k in range(nz):
+        target = (z + 1 + k) % nz
+        top_a, norm_a = stat_ref[y, target, 0], stat_ref[y, target, 1]
+        top_b, norm_b = y_stat[target, 0], y_stat[target, 1]
+        top = jnp.maximum(top_a, top_b)
+        keep_a, keep_b = jnp.exp(top_a - top), jnp.exp(top_b - top)
+        norm = keep_a * norm_a + keep_b * norm_b
+        rows_a, rows_b = spread(keep_a), spread(keep_b)
+        y_copies[k].wait_recv()
+        both = rows_a * sum_ref[y, target].astype(F32) + rows_b * y_sum[k].astype(F32)
+        if k < nz - 1:
+            c_sum[k] = both.astype(BF16)
+            c_stat[k, 0] = top
+            c_stat[k, 1] = norm
+            there = {"ctx": target * 2 + y}
+            for copy in (
+                remote(c_stat.at[k], z_stat.at[k], zt_send.at[k], zt_recv.at[k], there),
+                remote(c_sum.at[k], z_sum.at[k], zs_send.at[k], zs_recv.at[k], there),
+            ):
+                copy.start()
+                z_copies.append(copy)
+    for copy in z_copies[0::2]:
+        copy.wait_recv()
+    highest = top
+    for k in range(nz - 1):
+        highest = jnp.maximum(highest, z_stat[k, 0])
+    keep = jnp.exp(top - highest)
+    all_norm = keep * norm
+    factors = []
+    for k in range(nz - 1):
+        factors.append(jnp.exp(z_stat[k, 0] - highest))
+        all_norm = all_norm + factors[k] * z_stat[k, 1]
+    safe = jnp.where(all_norm > 0, all_norm, 1.0)
+    total = spread(keep / safe) * both
+    for k in range(nz - 1):
+        z_copies[2 * k + 1].wait_recv()
+        total = total + spread(factors[k] / safe) * z_sum[k].astype(F32)
+    wide[...] = total.reshape(requests, heads_here, latent)
+    outs = []
+    for h in range(heads_here):
+        outs.append(jnp.dot(wide[:, h, :].astype(BF16), value_ref[h], preferred_element_type=F32).astype(BF16))
+    head_out = jnp.concatenate(outs, axis=1)
+    load.wait()
+
+    aligned = block % 128 == 0
+    h_copies, p_copies = [], []
+
+    def place(k):
+        return (me + 1 + k) % ctx if aligned else k
+
+    def forward(k):
+        target = place(k)
+        h_copies[k].wait_recv()
+        merged = h_keep[k] + h_in[k]
+        if aligned:
+            p_out[k] = merged.astype(BF16)
+            if k < ctx - 1:
+                copy = remote(p_out.at[k], p_in.at[k], p_send.at[k], p_recv.at[k], {"ctx": target})
+                copy.start()
+                p_copies.append(copy)
+        else:
+            p_out[k] = merged.astype(BF16)
+
+            @pl.when(target != me)
+            def _():
+                slot = (target - me + ctx - 1) % ctx
+                remote(p_out.at[k], p_in.at[slot], p_send.at[slot], p_recv.at[slot], {"ctx": target}).start()
+
+    for k in range(ctx):
+        if aligned:
+            columns = weight[:, pl.ds(pl.multiple_of(place(k) * block, 128), block)]
+        else:
+            columns = weight[:, k * block:(k + 1) * block]
+        part = jnp.dot(head_out, columns, preferred_element_type=F32)
+        low, high = part[:, :half], part[:, half:]
+        h_keep[k] = jnp.where(core == 0, low, high)
+        h_out[k] = jnp.where(core == 0, high, low)
+        copy = remote(h_out.at[k], h_in.at[k], h_send.at[k], h_recv.at[k], twin)
+        copy.start()
+        h_copies.append(copy)
+        if k > 0:
+            forward(k - 1)
+    forward(ctx - 1)
+    if aligned:
+        result = h_keep[ctx - 1] + h_in[ctx - 1]
+    else:
+        result = p_out[me].astype(F32)
+    for k in range(ctx - 1):
+        remote(p_out.at[k], p_in.at[k], p_send.at[k], p_recv.at[k], partner).wait_recv()
+        result = result + p_in[k].astype(F32)
+    out_ref[...] = result.astype(BF16)
+    for k in range(ctx - 1):
+        remote(p_out.at[k], p_in.at[k], p_send.at[k], p_recv.at[k], partner).wait_send()
+    for copy in h_copies + z_copies + y_copies + [stat_copy]:
+        copy.wait_send()
+
+
+def project(sums, stats, value_absorb, output_weight, ctx):
+    nz = ctx // 2
+    _, _, rows, latent = sums.shape
+    heads_here = value_absorb.shape[0]
+    requests = rows // heads_here
+    half = output_weight.shape[1] // (2 * ctx)
+    vmem = pl.BlockSpec(memory_space=pltpu.VMEM)
+    dma = pltpu.SemaphoreType.DMA
+    stat_tail = stats.shape[2:]
+    return pl.pallas_call(
+        functools.partial(project_kernel, ctx),
+        out_shape=jax.ShapeDtypeStruct((requests, half), BF16),
+        in_specs=[vmem, vmem, vmem, pl.BlockSpec(memory_space=pl.ANY)],
+        out_specs=vmem,
+        scratch_shapes=[
+            pltpu.VMEM(output_weight.shape, BF16),
+            pltpu.VMEM((nz, rows, latent), BF16),
+            pltpu.VMEM((nz,) + stat_tail, F32),
+            pltpu.VMEM((nz - 1, rows, latent), BF16),
+            pltpu.VMEM((nz - 1,) + stat_tail, F32),
+            pltpu.VMEM((nz - 1, rows, latent), BF16),
+            pltpu.VMEM((nz - 1,) + stat_tail, F32),
+            pltpu.VMEM((requests, heads_here, latent), F32),
+            pltpu.VMEM((ctx, requests, half), F32),
+            pltpu.VMEM((ctx, requests, half), F32),
+            pltpu.VMEM((ctx, requests, half), F32),
+            pltpu.VMEM((ctx, requests, half), BF16),
+            pltpu.VMEM((ctx - 1, requests, half), BF16),
+            dma, dma((nz,)), dma((nz,)), dma, dma,
+            dma((nz - 1,)), dma((nz - 1,)), dma((nz - 1,)), dma((nz - 1,)),
+            dma((ctx,)), dma((ctx,)), dma((ctx - 1,)), dma((ctx - 1,)),
+        ],
+        compiler_params=pltpu.CompilerParams(collective_id=1, has_side_effects=True, vmem_limit_bytes=40 << 20),
+    )(sums, stats, value_absorb, output_weight)
+
+
+def body(ctx, query_nope, query_rope, key_absorb, value_absorb, output_weight, latent_cache, page_owner):
     requests, heads_here, nope_size = query_nope.shape
     latent_size = key_absorb.shape[2]
     rope_size = query_rope.shape[1] // heads_here
     score_scale = (nope_size + rope_size) ** (-0.5)
-    query_latent = jnp.einsum(
-        "rhn,hnl->rhl", query_nope, key_absorb, preferred_element_type=F32
-    ).astype(BF16)
-    query_mine = jnp.concatenate(
-        [query_latent, query_rope.reshape(requests, heads_here, rope_size)], axis=2
-    ).reshape(requests * heads_here, -1)
-    gathered = lax.all_gather(query_mine, "ctx", axis=0, tiled=False)
+    gathered = gather_queries(query_nope, query_rope, key_absorb, ctx)
     owners = jnp.where(page_owner < 0, requests, page_owner)
     sums, stats = attention(gathered, latent_cache, owners, requests, heads_here, latent_size, score_scale)
-    ctx = gathered.shape[0]
-    got_sum = lax.all_to_all(sums, "ctx", split_axis=0, concat_axis=0, tiled=True).reshape(
-        ctx, requests, heads_here, latent_size).astype(F32)
-    got_stat = lax.all_to_all(
-        stats.reshape(ctx, heads_here, -1), "ctx", split_axis=0, concat_axis=0, tiled=True)
-    got_max = got_stat[:, :, :requests].transpose(0, 2, 1)
-    got_total = got_stat[:, :, requests:2 * requests].transpose(0, 2, 1)
-    top_max = jnp.max(got_max, axis=0)
-    factor = jnp.exp(got_max - top_max[None])
-    mine_total = jnp.sum(factor * got_total, axis=0)
-    mine_sum = jnp.sum(factor[..., None] * got_sum, axis=0)
-    attended = (mine_sum / mine_total[..., None]).astype(BF16)
-    head_out = jnp.einsum(
-        "rhl,hlv->rhv", attended, value_absorb, preferred_element_type=F32
-    ).astype(BF16)
-    partial_out = jnp.dot(
-        head_out.reshape(requests, -1), output_weight, preferred_element_type=F32
-    )
-    return lax.psum_scatter(
-        partial_out.astype(BF16), ("ctx", "head"), scatter_dimension=1, tiled=True
-    )
+    return project(sums, stats, value_absorb, output_weight, ctx)
 
 
 def solution(mesh):
     return jax.shard_map(
-        body,
+        functools.partial(body, mesh.shape["ctx"]),
         mesh=mesh,
         in_specs=(
             P("groups", ("ctx", "head"), None),

time: 192 us -> 74.2 us (0.39)
  waiting for transfers between devices: 126 us -> 0 us
  Pallas kernels: 21.7 us -> 69.8 us
  between operations: 13.5 us -> 0.04 us
  blocking collectives: 9.89 us -> 0 us
  matrix products: 8.46 us -> 0 us
  local copies, waits for them, and re-layouts: 8.07 us -> 3.31 us
  starting transfers between devices: 3.6 us -> 0 us
    unnamed x3 -> x0, waiting for transfers between devices: 59.7 us -> none
    pallas_call x0 -> x2, Pallas kernels: none -> 49.1 us  [the longest x1 26.7 us: project(): pl.pallas_call(functools.partial(project_kernel, ctx), out_shape=jax.Shap...]
    all_gather x1 -> x0, waiting for transfers between devices: 44 us -> none  [body(): gathered = lax.all_gather(query_mine, 'ctx', axis=0, tiled=False)]
    all_to_all x1 -> x0, waiting for transfers between devices: 22.7 us -> none  [body(): lax.all_to_all(sums, 'ctx', split_axis=0, concat_axis=0, tiled=True)]
    all_to_all x1 -> x0, blocking collectives: 9.89 us -> none  [body(): lax.all_to_all(stats.reshape(ctx, heads_here, -1), 'ctx', split_axis=0, c...]
    dot_general x3 -> x0, matrix products: 8.46 us -> none  [the longest x1 7.2 us: body(): jnp.dot(head_out.reshape(requests, -1), output_weight, preferred_element_...]
    all_to_all x1 -> x0, starting transfers between devices: 3.56 us -> none  [body(): lax.all_to_all(sums, 'ctx', split_axis=0, concat_axis=0, tiled=True)]
    unnamed x8 -> x9, local copies, waits for them, and re-layouts: 4.44 us -> 3.31 us
  transfers between devices with their start and end apart: 3 -> 0, of which waited for: 3 -> 0; matrix products, arithmetic and copies ran while one was open for 0% -> 0% of each run, Pallas kernels for 0% -> 0%
where the time goes in v2:
time: 74.2 us; the launch traced here: 73.9 us
  Pallas kernels  69.8 us (94%)
  local copies, waits for them, and re-layouts  3.31 us (4%)
  other arithmetic  0.77 us (1%)
    pallas_call x1, Pallas kernels, project(): pl.pallas_call(functools.partial(project_kernel, ctx), out_shape=jax.Shap...  26.7 us
    pallas_call x1, Pallas kernels, gather_queries(): pl.pallas_call(functools.partial(gather_kernel, nz), out_shape=jax.ShapeD...  22.4 us
    pallas_call x1, Pallas kernels, attention(): pl.pallas_call(functools.partial(attention_kernel, heads_here, group, sco...  20.7 us
    unnamed x9, local copies, waits for them, and re-layouts  3.31 us

profile of v2, /device:TPU:0, one launch (start us, length us, event | category | flops | bytes accessed | tf_op | source)
XLA Modules:
  0.0 73.9 jit_solution(2875606657480296546)
XLA Ops:
  0.0 0.0 copy-start
  0.0 0.8 %compare_select_fusion.owner_ref = s32[224]{0:T(256)S(1)} fusion(s32[224]{0:T(256)} %param.13), kind=kLoop, calls=%fused_computation | loop fusion | flops 448 | bytes 1792 | tf_op jit(solution)/shard_map/jit(_where)/select_n | solution.py:418
  0.8 0.0 copy-start.1
  0.8 1.2 %copy-done.1 = bf16[8,128,512]{2,1,0:T(8,128)(2,1)S(1)} copy-done((bf16[8,128,512]{2,1,0:T(8,128)(2,1)S(1)}, bf16[8,128,512]{2,1,0:T(8,128)(2,1)}, u32[]{:S(2)}) %copy-start.1) | copy-done | bytes 1048600
  2.0 0.0 copy-start.2
  2.0 0.8 %copy-done.2 = bf16[16,8,128]{2,1,0:T(8,128)(2,1)S(1)} copy-done((bf16[16,8,128]{2,1,0:T(8,128)(2,1)S(1)}, bf16[16,8,128]{2,1,0:T(8,128)(2,1)}, u32[]{:S(2)}) %copy-start.2) | copy-done | bytes 32792
  2.8 0.0 copy-start.3
  2.8 0.7 copy-done.3
  3.5 22.4 %shard_map.73.q_ref = bf16[8,128,576]{2,1,0:T(8,128)(2,1)S(1)} custom-call(bf16[16,8,128]{2,1,0:T(8,128)(2,1)S(1)} %copy-done.2, bf16[16,512]{1,0:T(8,128)(2,1)S(1)} %copy-done.3, bf16[8,128,512]{2,1,0:T(8,128)(2,1)S(1)} %copy-done.1), custom_call_target="tpu_custom_call" | custom-call | tf_op jit(solution)/shard_map/pallas_call | solution.py:228
  25.9 20.7 %shard_map.74 = (bf16[2,4,128,512]{3,2,1,0:T(8,128)(2,1)S(1)}, f32[2,4,2,8,128]{4,3,2,1,0:T(8,128)S(1)}) custom-call(s32[224]{0:T(256)S(1)} %compare_select_fusion.owner_ref, bf16[8,128,576]{2,1,0:T(8,128)(2,1)S(1)} %shard_map.73.q_ref, bf16[224,64,576]{2,1,0:T(8,128)(2,1)} %cache_ref.1), custom_call_target="tpu_custom_call" | custom-call | tf_op jit(solution)/shard_map/pallas_call | solution.py:97
  46.6 0.0 copy-done
  46.6 26.7 %shard_map.75 = bf16[16,448]{1,0:T(8,128)(2,1)S(1)} custom-call(bf16[2,4,128,512]{3,2,1,0:T(8,128)(2,1)S(1)} %get-tuple-element.7.sum_ref, f32[2,4,2,8,128]{4,3,2,1,0:T(8,128)S(1)} %get-tuple-element.8.stat_ref, bf16[8,512,128]{2,1,0:T(8,128)(2,1)S(1)} %copy-done, bf16[1024,7168]{1,0:T(8,128)(2,1)} %weight_ref.1), custom_call_target="tpu_custom_call" | custom-call | tf_op jit(solution)/shard_map/pallas_call | solution.py:385
  73.3 0.6 copy.9
Async XLA Ops:
  0.0 46.6 %copy-start = (bf16[8,512,128]{2,1,0:T(8,128)(2,1)S(1)}, bf16[8,512,128]{2,1,0:T(8,128)(2,1)}, u32[]{:S(2)}) copy-start(bf16[8,512,128]{2,1,0:T(8,128)(2,1)} %value_ref.1) | copy-start | bytes 3145732
  0.8 1.2 %copy-start.1 = (bf16[8,128,512]{2,1,0:T(8,128)(2,1)S(1)}, bf16[8,128,512]{2,1,0:T(8,128)(2,1)}, u32[]{:S(2)}) copy-start(bf16[8,128,512]{2,1,0:T(8,128)(2,1)} %key_ref.1) | copy-start | bytes 3145732
  2.0 0.8 %copy-start.2 = (bf16[16,8,128]{2,1,0:T(8,128)(2,1)S(1)}, bf16[16,8,128]{2,1,0:T(8,128)(2,1)}, u32[]{:S(2)}) copy-start(bf16[16,8,128]{2,1,0:T(8,128)(2,1)} %nope_ref.1) | copy-start | bytes 98308
  2.8 0.7 copy-start.3

commit v3 on v2

--- a/solution.py
+++ b/solution.py
@@ -15,8 +15,8 @@
     return lax.dot_general(a, b, (((1,), (1,)), ((), ())), preferred_element_type=F32)
 
 
-def attention_kernel(heads_here, group, score_scale, owner_ref, q_ref, cache_ref, sum_ref, stat_ref,
-                     pages, query, scores, peak, total, acc, sems):
+def attention_kernel(heads_here, group, score_scale, owner_hbm, q_ref, cache_ref, sum_ref, stat_ref,
+                     owner_ref, owner_sem, pages, query, scores, peak, total, acc, sems):
     ctx = q_ref.shape[0]
     slots, heads, _ = acc.shape
     requests = slots - 1
@@ -29,6 +29,8 @@
         window = pl.ds(i * chunk, chunk)
         return pltpu.make_async_copy(cache_ref.at[window], pages.at[window], sems.at[i])
 
+    owner_load = pltpu.make_async_copy(owner_hbm, owner_ref, owner_sem)
+    owner_load.start()
     for i in range(chunks):
         fetch(i).start()
     for r in range(requests):
@@ -37,16 +39,18 @@
     peak[...] = jnp.full_like(peak, -1e30)
     total[...] = jnp.zeros_like(total)
     acc[...] = jnp.zeros_like(acc)
+    owner_load.wait()
+
+    def owner_of(page):
+        owner = owner_ref[page]
+        return jnp.where(owner < 0, requests, owner)
 
     def score_group(base):
-        found = []
+        owners = [owner_of(base + j) for j in range(group)]
         for j in range(group):
-            owner = owner_ref[base + j]
-            found.append(dot_nt(query[jnp.minimum(owner, requests - 1)], pages[base + j]) * score_scale)
-        for j in range(group):
-            owner = owner_ref[base + j]
-            scores[base + j] = found[j]
-            peak[owner] = jnp.maximum(peak[owner], found[j])
+            found = dot_nt(query[jnp.minimum(owners[j], requests - 1)], pages[base + j]) * score_scale
+            scores[base + j] = found
+            peak[owners[j]] = jnp.maximum(peak[owners[j]], found)
 
     @pl.loop(0, chunks)
     def _(i):
@@ -62,15 +66,15 @@
     @pl.loop(0, page_count // group)
     def _(g):
         base = g * group
-        parts = []
+        owners = [owner_of(base + j) for j in range(group)]
+        weights = []
         for j in range(group):
-            owner = owner_ref[base + j]
-            weight = jnp.exp(scores[base + j] - peak[owner])
-            total[owner] = total[owner] + weight
-            parts.append(jnp.dot(weight.astype(BF16), pages[base + j, :, :latent], preferred_element_type=F32))
+            weight = jnp.exp(scores[base + j] - peak[owners[j]])
+            total[owners[j]] = total[owners[j]] + weight
+            weights.append(weight.astype(BF16))
         for j in range(group):
-            owner = owner_ref[base + j]
-            acc[owner] = acc[owner] + parts[j]
+            acc[owners[j]] = acc[owners[j]] + jnp.dot(
+                weights[j], pages[base + j, :, :latent], preferred_element_type=F32)
 
     lane = lax.broadcasted_iota(jnp.int32, (heads, stat_ref.shape[-1]), 1)
     top = jnp.zeros(lane.shape, F32)
@@ -93,30 +97,26 @@
     sum_shape = (2, ctx // 2, requests * heads_here, latent)
     stat_shape = (2, ctx // 2, 2, heads_here, 128)
     chunks = next(n for n in (14, 8, 7, 4, 2, 1) if page_count % n == 0)
-    group = next(n for n in (8, 4, 2, 1) if (page_count // chunks) % n == 0)
+    group = next(n for n in (16, 8, 4, 2, 1) if (page_count // chunks) % n == 0)
     return pl.pallas_call(
         functools.partial(attention_kernel, heads_here, group, score_scale),
-        grid_spec=pltpu.PrefetchScalarGridSpec(
-            num_scalar_prefetch=1,
-            grid=(1,),
-            in_specs=[
-                pl.BlockSpec(gathered.shape, lambda i, o: (0, 0, 0), pipeline_mode=pl.Buffered(1)),
-                pl.BlockSpec(memory_space=pl.ANY),
-            ],
-            out_specs=[
-                pl.BlockSpec(sum_shape, lambda i, o: (0,) * 4, pipeline_mode=pl.Buffered(1)),
-                pl.BlockSpec(stat_shape, lambda i, o: (0,) * 5, pipeline_mode=pl.Buffered(1)),
-            ],
-            scratch_shapes=[
-                pltpu.VMEM((page_count, page_len, entry), BF16),
-                pltpu.VMEM((requests, heads, entry), BF16),
-                pltpu.VMEM((page_count, heads, page_len), F32),
-                pltpu.VMEM((requests + 1, heads, page_len), F32),
-                pltpu.VMEM((requests + 1, heads, page_len), F32),
-                pltpu.VMEM((requests + 1, heads, latent), F32),
-                pltpu.SemaphoreType.DMA((chunks,)),
-            ],
-        ),
+        in_specs=[
+            pl.BlockSpec(memory_space=pltpu.HBM),
+            pl.BlockSpec(memory_space=pltpu.VMEM),
+            pl.BlockSpec(memory_space=pltpu.HBM),
+        ],
+        out_specs=[pl.BlockSpec(memory_space=pltpu.VMEM)] * 2,
+        scratch_shapes=[
+            pltpu.SMEM((page_count,), jnp.int32),
+            pltpu.SemaphoreType.DMA,
+            pltpu.VMEM((page_count, page_len, entry), BF16),
+            pltpu.VMEM((requests, heads, entry), BF16),
+            pltpu.VMEM((page_count, heads, page_len), F32),
+            pltpu.VMEM((requests + 1, heads, page_len), F32),
+            pltpu.VMEM((requests + 1, heads, page_len), F32),
+            pltpu.VMEM((requests + 1, heads, latent), F32),
+            pltpu.SemaphoreType.DMA((chunks,)),
+        ],
         out_shape=[
             jax.ShapeDtypeStruct(sum_shape, BF16),
             jax.ShapeDtypeStruct(stat_shape, F32),
@@ -131,7 +131,7 @@
         device_id=where, device_id_type=pl.DeviceIdType.MESH)
 
 
-def gather_kernel(nz, nope_ref, rope_ref, key_ref, out_ref, wide, rows, mine,
+def gather_kernel(nz, nope_hbm, rope_hbm, key_hbm, out_ref, nope_ref, rope_ref, key_ref, in_sems, wide, rows, mine,
                   y_send, y_recv, up_send, up_recv, down_send, down_recv):
     requests, heads_here, _ = nope_ref.shape
     latent = key_ref.shape[2]
@@ -141,6 +141,12 @@
     partner = {"ctx": z * 2 + 1 - y}
     above, below = {"ctx": me + 2}, {"ctx": me - 2}
     has_above, has_below = z + 1 < nz, z > 0
+    loads = [
+        pltpu.make_async_copy(src, dst, in_sems.at[i])
+        for i, (src, dst) in enumerate(((nope_hbm, nope_ref), (rope_hbm, rope_ref), (key_hbm, key_ref)))
+    ]
+    for load in loads:
+        load.start()
 
     barrier = pltpu.get_barrier_semaphore()
     pl.semaphore_signal(barrier, inc=1, device_id=partner, device_id_type=pl.DeviceIdType.MESH)
@@ -153,6 +159,8 @@
     def _():
         pl.semaphore_signal(barrier, inc=1, device_id=below, device_id_type=pl.DeviceIdType.MESH)
 
+    for load in loads:
+        load.wait()
     wide[...] = nope_ref[...].astype(F32)
     for h in range(heads_here):
         rows[:, h, :latent] = jnp.dot(wide[:, h, :].astype(BF16), key_ref[h], preferred_element_type=F32)
@@ -228,9 +236,13 @@
     return pl.pallas_call(
         functools.partial(gather_kernel, nz),
         out_shape=jax.ShapeDtypeStruct((ctx, requests * heads_here, entry), BF16),
-        in_specs=[vmem] * 3,
+        in_specs=[pl.BlockSpec(memory_space=pltpu.HBM)] * 3,
         out_specs=vmem,
         scratch_shapes=[
+            pltpu.VMEM(query_nope.shape, BF16),
+            pltpu.VMEM(query_rope.shape, BF16),
+            pltpu.VMEM(key_absorb.shape, BF16),
+            dma((3,)),
             pltpu.VMEM(query_nope.shape, F32),
             pltpu.VMEM((requests, heads_here, entry), F32),
             pltpu.VMEM((requests * heads_here, entry), BF16),
@@ -240,16 +252,15 @@
     )(query_nope, query_rope, key_absorb)
 
 
-def project_kernel(ctx, sum_ref, stat_ref, value_ref, weight_ref, out_ref,
-                   weight, y_sum, y_stat, c_sum, c_stat, z_sum, z_stat, wide,
+def project_kernel(ctx, sum_ref, stat_ref, value_hbm, weight_ref, out_ref,
+                   weight, value_ref, value_sem, y_sum, y_stat, c_sum, c_stat, z_sum, z_stat, wide,
                    h_keep, h_out, h_in, p_out, p_in,
                    w_sem, ys_send, ys_recv, yt_send, yt_recv, zs_send, zs_recv, zt_send, zt_recv,
                    h_send, h_recv, p_send, p_recv):
     nz = ctx // 2
     requests, half = out_ref.shape
     block = 2 * half
-    heads_here = value_ref.shape[0]
-    latent = value_ref.shape[1]
+    heads_here, latent, _ = value_ref.shape
     me, core = lax.axis_index("ctx"), lax.axis_index("head")
     z, y = me // 2, me % 2
     partner, twin = {"ctx": z * 2 + 1 - y}, {"head": 1 - core}
@@ -259,6 +270,8 @@
         pl.semaphore_signal(barrier, inc=1, device_id={"ctx": (me + k) % ctx}, device_id_type=pl.DeviceIdType.MESH)
     pl.semaphore_signal(barrier, inc=1, device_id=twin, device_id_type=pl.DeviceIdType.MESH)
     load = pltpu.make_async_copy(weight_ref, weight, w_sem)
+    value_load = pltpu.make_async_copy(value_hbm, value_ref, value_sem)
+    value_load.start()
     load.start()
     pl.semaphore_wait(barrier, ctx)
 
@@ -315,6 +328,7 @@
         total = total + spread(factors[k] / safe) * z_sum[k].astype(F32)
     wide[...] = total.reshape(requests, heads_here, latent)
     outs = []
+    value_load.wait()
     for h in range(heads_here):
         outs.append(jnp.dot(wide[:, h, :].astype(BF16), value_ref[h], preferred_element_type=F32).astype(BF16))
     head_out = jnp.concatenate(outs, axis=1)
@@ -385,10 +399,12 @@
     return pl.pallas_call(
         functools.partial(project_kernel, ctx),
         out_shape=jax.ShapeDtypeStruct((requests, half), BF16),
-        in_specs=[vmem, vmem, vmem, pl.BlockSpec(memory_space=pl.ANY)],
+        in_specs=[vmem, vmem] + [pl.BlockSpec(memory_space=pltpu.HBM)] * 2,
         out_specs=vmem,
         scratch_shapes=[
             pltpu.VMEM(output_weight.shape, BF16),
+            pltpu.VMEM(value_absorb.shape, BF16),
+            dma,
             pltpu.VMEM((nz, rows, latent), BF16),
             pltpu.VMEM((nz,) + stat_tail, F32),
             pltpu.VMEM((nz - 1, rows, latent), BF16),
@@ -414,9 +430,10 @@
     latent_size = key_absorb.shape[2]
     rope_size = query_rope.shape[1] // heads_here
     score_scale = (nope_size + rope_size) ** (-0.5)
+    query_nope, query_rope, key_absorb, page_owner = (
+        pltpu.with_memory_space_constraint(x, pltpu.HBM) for x in (query_nope, query_rope, key_absorb, page_owner))
     gathered = gather_queries(query_nope, query_rope, key_absorb, ctx)
-    owners = jnp.where(page_owner < 0, requests, page_owner)
-    sums, stats = attention(gathered, latent_cache, owners, requests, heads_here, latent_size, score_scale)
+    sums, stats = attention(gathered, latent_cache, page_owner, requests, heads_here, latent_size, score_scale)
     return project(sums, stats, value_absorb, output_weight, ctx)
 
 

time: 74.2 us -> 67 us (0.903)
  Pallas kernels: 69.8 us -> 66.3 us
  local copies, waits for them, and re-layouts: 3.31 us -> 0.61 us
  other arithmetic: 0.77 us -> 0 us
    pallas_call x1, Pallas kernels: 20.7 us -> 16 us  [attention(): pl.pallas_call(functools.partial(attention_kernel, heads_here, group, sco...]
    unnamed x9 -> x3, local copies, waits for them, and re-layouts: 3.31 us -> 0.61 us
    pallas_call x1, Pallas kernels: 22.4 us -> 24 us  [gather_queries(): pl.pallas_call(functools.partial(gather_kernel, nz), out_shape=jax.ShapeD...]
    select_n x1 -> x0, other arithmetic: 0.77 us -> none  [body(): owners = jnp.where(page_owner < 0, requests, page_owner)]
where the time goes in v3:
time: 67 us; the launch traced here: 66.9 us
  Pallas kernels  66.3 us (99%)
    pallas_call x1, Pallas kernels, project(): pl.pallas_call(functools.partial(project_kernel, ctx), out_shape=jax.Shap...  26.3 us
    pallas_call x1, Pallas kernels, gather_queries(): pl.pallas_call(functools.partial(gather_kernel, nz), out_shape=jax.ShapeD...  24 us
    pallas_call x1, Pallas kernels, attention(): pl.pallas_call(functools.partial(attention_kernel, heads_here, group, sco...  16 us

profile of v3, /device:TPU:0, one launch (start us, length us, event | category | flops | bytes accessed | tf_op | source)
XLA Modules:
  0.0 66.9 jit_solution(7910734886659891560)
XLA Ops:
  0.0 0.0 copy-start
  0.0 24.0 %shard_map.73.q_ref = bf16[8,128,576]{2,1,0:T(8,128)(2,1)S(1)} custom-call(bf16[16,8,128]{2,1,0:T(8,128)(2,1)} %nope_hbm.1, bf16[16,512]{1,0:T(8,128)(2,1)} %rope_hbm.1, bf16[8,128,512]{2,1,0:T(8,128)(2,1)} %key_hbm.1), custom_call_target="tpu_custom_call" | custom-call | tf_op jit(solution)/shard_map/pallas_call | solution.py:236
  24.0 16.0 %shard_map.74 = (bf16[2,4,128,512]{3,2,1,0:T(8,128)(2,1)S(1)}, f32[2,4,2,8,128]{4,3,2,1,0:T(8,128)S(1)}) custom-call(s32[224]{0:T(256)} %owner_hbm.1, bf16[8,128,576]{2,1,0:T(8,128)(2,1)S(1)} %shard_map.73.q_ref, bf16[224,64,576]{2,1,0:T(8,128)(2,1)} %cache_ref.1), custom_call_target="tpu_custom_call" | custom-call | tf_op jit(solution)/shard_map/pallas_call | solution.py:101
  40.0 0.0 copy-done
  40.0 26.3 %shard_map.75 = bf16[16,448]{1,0:T(8,128)(2,1)S(1)} custom-call(bf16[2,4,128,512]{3,2,1,0:T(8,128)(2,1)S(1)} %get-tuple-element.7.sum_ref, f32[2,4,2,8,128]{4,3,2,1,0:T(8,128)S(1)} %get-tuple-element.8.stat_ref, bf16[8,512,128]{2,1,0:T(8,128)(2,1)S(1)} %copy-done, bf16[1024,7168]{1,0:T(8,128)(2,1)} %weight_ref.1), custom_call_target="tpu_custom_call" | custom-call | tf_op jit(solution)/shard_map/pallas_call | solution.py:399
  66.3 0.6 copy.9
Async XLA Ops:
  0.0 40.0 %copy-start = (bf16[8,512,128]{2,1,0:T(8,128)(2,1)S(1)}, bf16[8,512,128]{2,1,0:T(8,128)(2,1)}, u32[]{:S(2)}) copy-start(bf16[8,512,128]{2,1,0:T(8,128)(2,1)} %value_hbm.1) | copy-start | bytes 3145732

commit v4 on v3

--- a/solution.py
+++ b/solution.py
@@ -7,6 +7,7 @@
 from jax.experimental.pallas import tpu as pltpu
 from jax.sharding import PartitionSpec as P
 
+PARTS = 2
 F32 = jnp.float32
 BF16 = jnp.bfloat16
 
@@ -171,60 +172,69 @@
 
     pl.semaphore_wait(barrier, 1 + has_above.astype(jnp.int32) + has_below.astype(jnp.int32))
 
-    def across(origin, src):
-        slot = out_ref.at[origin * 2 + y]
-        return remote(slot if src is None else src, slot, y_send.at[origin], y_recv.at[origin], partner)
-
-    def upward(step, src=None):
-        slot = out_ref.at[me - 2 * step]
-        return remote(slot if src is None else src, slot, up_send.at[step], up_recv.at[step], above)
-
-    def downward(step, src=None):
-        slot = out_ref.at[me + 2 * step]
-        return remote(slot if src is None else src, slot, down_send.at[step], down_recv.at[step], below)
-
-    def arrival(slot, sem):
+    depth = mine.shape[0] // PARTS
+
+    def block(ref, part):
+        return ref.at[part * depth:(part + 1) * depth]
+
+    def across(origin, part, src=None):
+        slot, i = block(out_ref.at[origin * 2 + y], part), origin * PARTS + part
+        return remote(slot if src is None else block(src, part), slot, y_send.at[i], y_recv.at[i], partner)
+
+    def upward(step, part, src=None):
+        slot, i = block(out_ref.at[me - 2 * step], part), step * PARTS + part
+        return remote(slot if src is None else block(src, part), slot, up_send.at[i], up_recv.at[i], above)
+
+    def downward(step, part, src=None):
+        slot, i = block(out_ref.at[me + 2 * step], part), step * PARTS + part
+        return remote(slot if src is None else block(src, part), slot, down_send.at[i], down_recv.at[i], below)
+
+    def arrival(row, part, sem):
+        slot = block(out_ref.at[row], part)
         return remote(slot, slot, sem, sem, partner)
 
-    @pl.when(has_above)
-    def _():
-        upward(0, mine).start()
-
-    @pl.when(has_below)
-    def _():
-        downward(0, mine).start()
-
-    across(z, mine).start()
+    for part in range(PARTS):
+        @pl.when(has_above)
+        def _():
+            upward(0, part, mine).start()
+
+        @pl.when(has_below)
+        def _():
+            downward(0, part, mine).start()
+
+        across(z, part, mine).start()
     for step in range(nz - 1):
-        @pl.when(z - 1 - step >= 0)
-        def _():
-            arrival(out_ref.at[me - 2 * (step + 1)], up_recv.at[step]).wait_recv()
-            if step + 1 < nz - 1:
-                @pl.when(has_above)
-                def _():
-                    upward(step + 1).start()
-            across(z - 1 - step, None).start()
-
-        @pl.when(z + 1 + step < nz)
-        def _():
-            arrival(out_ref.at[me + 2 * (step + 1)], down_recv.at[step]).wait_recv()
-            if step + 1 < nz - 1:
-                @pl.when(has_below)
-                def _():
-                    downward(step + 1).start()
-            across(z + 1 + step, None).start()
-
-    for origin in range(nz):
-        across(origin, mine).wait_send()
-        arrival(out_ref.at[origin * 2 + 1 - y], y_recv.at[origin]).wait_recv()
-    for step in range(nz - 1):
-        @pl.when(has_above & (z - step >= 0))
-        def _():
-            upward(step, mine).wait_send()
-
-        @pl.when(has_below & (z + step < nz))
-        def _():
-            downward(step, mine).wait_send()
+        for part in range(PARTS):
+            @pl.when(z - 1 - step >= 0)
+            def _():
+                arrival(me - 2 * (step + 1), part, up_recv.at[step * PARTS + part]).wait_recv()
+                if step + 1 < nz - 1:
+                    @pl.when(has_above)
+                    def _():
+                        upward(step + 1, part).start()
+                across(z - 1 - step, part).start()
+
+            @pl.when(z + 1 + step < nz)
+            def _():
+                arrival(me + 2 * (step + 1), part, down_recv.at[step * PARTS + part]).wait_recv()
+                if step + 1 < nz - 1:
+                    @pl.when(has_below)
+                    def _():
+                        downward(step + 1, part).start()
+                across(z + 1 + step, part).start()
+
+    for part in range(PARTS):
+        for origin in range(nz):
+            across(origin, part, mine).wait_send()
+            arrival(origin * 2 + 1 - y, part, y_recv.at[origin * PARTS + part]).wait_recv()
+        for step in range(nz - 1):
+            @pl.when(has_above & (z - step >= 0))
+            def _():
+                upward(step, part, mine).wait_send()
+
+            @pl.when(has_below & (z + step < nz))
+            def _():
+                downward(step, part, mine).wait_send()
 
 
 def gather_queries(query_nope, query_rope, key_absorb, ctx):
@@ -246,7 +256,8 @@
             pltpu.VMEM(query_nope.shape, F32),
             pltpu.VMEM((requests, heads_here, entry), F32),
             pltpu.VMEM((requests * heads_here, entry), BF16),
-            dma((nz,)), dma((nz,)), dma((nz,)), dma((nz,)), dma((nz,)), dma((nz,)),
+            dma((nz * PARTS,)), dma((nz * PARTS,)), dma((nz * PARTS,)),
+            dma((nz * PARTS,)), dma((nz * PARTS,)), dma((nz * PARTS,)),
         ],
         compiler_params=pltpu.CompilerParams(collective_id=0, has_side_effects=True, vmem_limit_bytes=16 << 20),
     )(query_nope, query_rope, key_absorb)
@@ -275,20 +286,28 @@
     load.start()
     pl.semaphore_wait(barrier, ctx)
 
+    depth = y_sum.shape[1] // PARTS
+
+    def lines(part):
+        return slice(part * depth, (part + 1) * depth)
+
     stat_copy = remote(stat_ref.at[1 - y], y_stat, yt_send, yt_recv, partner)
     stat_copy.start()
     y_copies = []
     for k in range(nz):
         target = (z + 1 + k) % nz
-        copy = remote(sum_ref.at[1 - y, target], y_sum.at[k], ys_send.at[k], ys_recv.at[k], partner)
-        copy.start()
-        y_copies.append(copy)
+        for part in range(PARTS):
+            i = k * PARTS + part
+            copy = remote(sum_ref.at[1 - y, target, lines(part)], y_sum.at[k, lines(part)],
+                          ys_send.at[i], ys_recv.at[i], partner)
+            copy.start()
+            y_copies.append(copy)
     stat_copy.wait_recv()
 
     def spread(factor):
         return jnp.concatenate([factor[:, r:r + 1] for r in range(requests)], axis=0)
 
-    z_copies = []
+    z_copies, z_stats = [], []
     for k in range(nz):
         target = (z + 1 + k) % nz
         top_a, norm_a = stat_ref[y, target, 0], stat_ref[y, target, 1]
@@ -297,20 +316,26 @@
         keep_a, keep_b = jnp.exp(top_a - top), jnp.exp(top_b - top)
         norm = keep_a * norm_a + keep_b * norm_b
         rows_a, rows_b = spread(keep_a), spread(keep_b)
-        y_copies[k].wait_recv()
-        both = rows_a * sum_ref[y, target].astype(F32) + rows_b * y_sum[k].astype(F32)
+        there = {"ctx": target * 2 + y}
         if k < nz - 1:
-            c_sum[k] = both.astype(BF16)
             c_stat[k, 0] = top
             c_stat[k, 1] = norm
-            there = {"ctx": target * 2 + y}
-            for copy in (
-                remote(c_stat.at[k], z_stat.at[k], zt_send.at[k], zt_recv.at[k], there),
-                remote(c_sum.at[k], z_sum.at[k], zs_send.at[k], zs_recv.at[k], there),
-            ):
+            copy = remote(c_stat.at[k], z_stat.at[k], zt_send.at[k], zt_recv.at[k], there)
+            copy.start()
+            z_stats.append(copy)
+        both = []
+        for part in range(PARTS):
+            i = k * PARTS + part
+            y_copies[i].wait_recv()
+            both.append(rows_a[lines(part)] * sum_ref[y, target, lines(part)].astype(F32)
+                        + rows_b[lines(part)] * y_sum[k, lines(part)].astype(F32))
+            if k < nz - 1:
+                c_sum[k, lines(part)] = both[part].astype(BF16)
+                copy = remote(c_sum.at[k, lines(part)], z_sum.at[k, lines(part)], zs_send.at[i], zs_recv.at[i], there)
                 copy.start()
                 z_copies.append(copy)
-    for copy in z_copies[0::2]:
+    both = jnp.concatenate(both, axis=0)
+    for copy in z_stats:
         copy.wait_recv()
     highest = top
     for k in range(nz - 1):
@@ -324,7 +349,8 @@
     safe = jnp.where(all_norm > 0, all_norm, 1.0)
     total = spread(keep / safe) * both
     for k in range(nz - 1):
-        z_copies[2 * k + 1].wait_recv()
+        for part in range(PARTS):
+            z_copies[k * PARTS + part].wait_recv()
         total = total + spread(factors[k] / safe) * z_sum[k].astype(F32)
     wide[...] = total.reshape(requests, heads_here, latent)
     outs = []
@@ -383,7 +409,7 @@
     out_ref[...] = result.astype(BF16)
     for k in range(ctx - 1):
         remote(p_out.at[k], p_in.at[k], p_send.at[k], p_recv.at[k], partner).wait_send()
-    for copy in h_copies + z_copies + y_copies + [stat_copy]:
+    for copy in h_copies + z_copies + z_stats + y_copies + [stat_copy]:
         copy.wait_send()
 
 
@@ -417,8 +443,8 @@
             pltpu.VMEM((ctx, requests, half), F32),
             pltpu.VMEM((ctx, requests, half), BF16),
             pltpu.VMEM((ctx - 1, requests, half), BF16),
-            dma, dma((nz,)), dma((nz,)), dma, dma,
-            dma((nz - 1,)), dma((nz - 1,)), dma((nz - 1,)), dma((nz - 1,)),
+            dma, dma((nz * PARTS,)), dma((nz * PARTS,)), dma, dma,
+            dma(((nz - 1) * PARTS,)), dma(((nz - 1) * PARTS,)), dma((nz - 1,)), dma((nz - 1,)),
             dma((ctx,)), dma((ctx,)), dma((ctx - 1,)), dma((ctx - 1,)),
         ],
         compiler_params=pltpu.CompilerParams(collective_id=1, has_side_effects=True, vmem_limit_bytes=40 << 20),

time: 67 us -> 64.7 us (0.966)
  Pallas kernels: 66.3 us -> 63.9 us
    pallas_call x1, Pallas kernels: 24 us -> 21.6 us  [gather_queries(): pl.pallas_call(functools.partial(gather_kernel, nz), out_shape=jax.ShapeD...]
where the time goes in v4:
time: 64.7 us; the launch traced here: 64.5 us
  Pallas kernels  63.9 us (99%)
    pallas_call x1, Pallas kernels, project(): pl.pallas_call(functools.partial(project_kernel, ctx), out_shape=jax.Shap...  26.3 us
    pallas_call x1, Pallas kernels, gather_queries(): pl.pallas_call(functools.partial(gather_kernel, nz), out_shape=jax.ShapeD...  21.6 us
    pallas_call x1, Pallas kernels, attention(): pl.pallas_call(functools.partial(attention_kernel, heads_here, group, sco...  15.9 us

profile of v4, /device:TPU:0, one launch (start us, length us, event | category | flops | bytes accessed | tf_op | source)
XLA Modules:
  0.0 64.5 jit_solution(12186403345884318316)
XLA Ops:
  0.0 0.0 copy-start
  0.0 21.6 %shard_map.73.q_ref = bf16[8,128,576]{2,1,0:T(8,128)(2,1)S(1)} custom-call(bf16[16,8,128]{2,1,0:T(8,128)(2,1)} %nope_hbm.1, bf16[16,512]{1,0:T(8,128)(2,1)} %rope_hbm.1, bf16[8,128,512]{2,1,0:T(8,128)(2,1)} %key_hbm.1), custom_call_target="tpu_custom_call" | custom-call | tf_op jit(solution)/shard_map/pallas_call | solution.py:246
  21.6 15.9 %shard_map.74 = (bf16[2,4,128,512]{3,2,1,0:T(8,128)(2,1)S(1)}, f32[2,4,2,8,128]{4,3,2,1,0:T(8,128)S(1)}) custom-call(s32[224]{0:T(256)} %owner_hbm.1, bf16[8,128,576]{2,1,0:T(8,128)(2,1)S(1)} %shard_map.73.q_ref, bf16[224,64,576]{2,1,0:T(8,128)(2,1)} %cache_ref.1), custom_call_target="tpu_custom_call" | custom-call | tf_op jit(solution)/shard_map/pallas_call | solution.py:102
  37.6 0.0 copy-done
  37.6 26.3 %shard_map.75 = bf16[16,448]{1,0:T(8,128)(2,1)S(1)} custom-call(bf16[2,4,128,512]{3,2,1,0:T(8,128)(2,1)S(1)} %get-tuple-element.7.sum_ref, f32[2,4,2,8,128]{4,3,2,1,0:T(8,128)S(1)} %get-tuple-element.8.stat_ref, bf16[8,512,128]{2,1,0:T(8,128)(2,1)S(1)} %copy-done, bf16[1024,7168]{1,0:T(8,128)(2,1)} %weight_ref.1), custom_call_target="tpu_custom_call" | custom-call | tf_op jit(solution)/shard_map/pallas_call | solution.py:425
  63.9 0.6 copy.9
Async XLA Ops:
  0.0 37.6 %copy-start = (bf16[8,512,128]{2,1,0:T(8,128)(2,1)S(1)}, bf16[8,512,128]{2,1,0:T(8,128)(2,1)}, u32[]{:S(2)}) copy-start(bf16[8,512,128]{2,1,0:T(8,128)(2,1)} %value_hbm.1) | copy-start | bytes 3145732

commit v5 on v4

--- a/solution.py
+++ b/solution.py
@@ -7,7 +7,7 @@
 from jax.experimental.pallas import tpu as pltpu
 from jax.sharding import PartitionSpec as P
 
-PARTS = 2
+PARTS = 4
 F32 = jnp.float32
 BF16 = jnp.bfloat16
 

time: 64.7 us -> 65.3 us (level)
    pallas_call x1, Pallas kernels: 26.3 us -> 28.1 us  [project(): pl.pallas_call(functools.partial(project_kernel, ctx), out_shape=jax.Shap...]
    pallas_call x1, Pallas kernels: 21.6 us -> 20.4 us  [gather_queries(): pl.pallas_call(functools.partial(gather_kernel, nz), out_shape=jax.ShapeD...]
where the time goes in v5:
time: 65.3 us; the launch traced here: 65.2 us
  Pallas kernels  64.5 us (99%)
    pallas_call x1, Pallas kernels, project(): pl.pallas_call(functools.partial(project_kernel, ctx), out_shape=jax.Shap...  28.1 us
    pallas_call x1, Pallas kernels, gather_queries(): pl.pallas_call(functools.partial(gather_kernel, nz), out_shape=jax.ShapeD...  20.4 us
    pallas_call x1, Pallas kernels, attention(): pl.pallas_call(functools.partial(attention_kernel, heads_here, group, sco...  15.9 us

profile of v5, /device:TPU:0, one launch (start us, length us, event | category | flops | bytes accessed | tf_op | source)
XLA Modules:
  0.0 65.2 jit_solution(2338263970866071989)
XLA Ops:
  0.0 0.0 copy-start
  0.0 20.4 %shard_map.73.q_ref = bf16[8,128,576]{2,1,0:T(8,128)(2,1)S(1)} custom-call(bf16[16,8,128]{2,1,0:T(8,128)(2,1)} %nope_hbm.1, bf16[16,512]{1,0:T(8,128)(2,1)} %rope_hbm.1, bf16[8,128,512]{2,1,0:T(8,128)(2,1)} %key_hbm.1), custom_call_target="tpu_custom_call" | custom-call | tf_op jit(solution)/shard_map/pallas_call | solution.py:246
  20.4 15.9 %shard_map.74 = (bf16[2,4,128,512]{3,2,1,0:T(8,128)(2,1)S(1)}, f32[2,4,2,8,128]{4,3,2,1,0:T(8,128)S(1)}) custom-call(s32[224]{0:T(256)} %owner_hbm.1, bf16[8,128,576]{2,1,0:T(8,128)(2,1)S(1)} %shard_map.73.q_ref, bf16[224,64,576]{2,1,0:T(8,128)(2,1)} %cache_ref.1), custom_call_target="tpu_custom_call" | custom-call | tf_op jit(solution)/shard_map/pallas_call | solution.py:102
  36.4 0.0 copy-done
  36.4 28.1 %shard_map.75 = bf16[16,448]{1,0:T(8,128)(2,1)S(1)} custom-call(bf16[2,4,128,512]{3,2,1,0:T(8,128)(2,1)S(1)} %get-tuple-element.7.sum_ref, f32[2,4,2,8,128]{4,3,2,1,0:T(8,128)S(1)} %get-tuple-element.8.stat_ref, bf16[8,512,128]{2,1,0:T(8,128)(2,1)S(1)} %copy-done, bf16[1024,7168]{1,0:T(8,128)(2,1)} %weight_ref.1), custom_call_target="tpu_custom_call" | custom-call | tf_op jit(solution)/shard_map/pallas_call | solution.py:425
  64.6 0.6 copy.9
Async XLA Ops:
  0.0 36.4 %copy-start = (bf16[8,512,128]{2,1,0:T(8,128)(2,1)S(1)}, bf16[8,512,128]{2,1,0:T(8,128)(2,1)}, u32[]{:S(2)}) copy-start(bf16[8,512,128]{2,1,0:T(8,128)(2,1)} %value_hbm.1) | copy-start | bytes 3145732
